TPU v7x, 32 devices: a whole 2x2x4 slice. The times are simulated.
32 devices in a mesh: shard: 4 (over y, x), mp: 4 (over z), segment: 2 (over core).
Axes of the slice: x: 2, y: 2, z: 4, core: 2. Of those that a mesh axis runs over, the one named last changes fastest.
Arguments:
- store_tokens: int32 [256, 48], P('shard'), may hold values from 0 to 16383
- retrieved: int32 [4, 12], replicated, may hold values from 0 to 63
- owner_shard: int32 [48, 1], replicated, may hold values from 0 to 3; in each aligned block of 12 rows (0 to 11, 12 to 23, ...) at most 3 rows name the same one
- targets: int32 [4, 64], P('shard'), may hold values from 0 to 16383
- vocab_table: bfloat16 [16384, 4096], P(None, ('mp', 'segment')), may hold values from -6 to 6
- norm_gains: float32 [3, 4096], replicated, may hold values from 0.1 to 1.9
- layer_weights: bfloat16 [2, 4, 4096, 4096], P('segment', None, 'shard', 'mp'), may hold values from -0.09375 to 0.09375
Outputs:
- encoded: bfloat16 [2304, 4096], P('shard', ('mp', 'segment'))
- decoded: bfloat16 [256, 4096], P('shard', ('mp', 'segment'))
Inputs may be any that keep to these rules, and one draw needn't show every extreme that they name: `owner_shard`: within the 12 passages of one question no shard owns more than 3; in every draw some question has exactly 3 passages from one shard.
All inputs are finite; a program needn't handle non-finite values.
Results may differ from a plain program's by a relative error of at most 0.015.
Values may be sent and summed in bfloat16 or wider, within the bound.
A program may use at most 128 MiB of HBM per device.

v0:
```python
import jax
import jax.numpy as jnp
from jax import lax
from jax.sharding import PartitionSpec as P

D = 4096
DH = 64
epsilon = 1e-06


def attend(query_rows, key_rows, value_rows, head_count):
    batch_size = query_rows.shape[0]
    head_size = query_rows.shape[2] // head_count
    query_heads = query_rows.reshape(batch_size, query_rows.shape[1], head_count, head_size)
    key_heads = key_rows.reshape(batch_size, key_rows.shape[1], head_count, head_size)
    value_heads = value_rows.reshape(batch_size, value_rows.shape[1], head_count, head_size)
    scores = jnp.einsum(
        "brhd,bshd->bhrs", query_heads, key_heads, preferred_element_type=jnp.float32
    ) * head_size ** (-0.5)
    shifted = jnp.exp(scores - jnp.max(scores, axis=-1, keepdims=True))
    attention = (shifted / jnp.sum(shifted, axis=-1, keepdims=True)).astype(jnp.bfloat16)
    mixture = jnp.einsum(
        "bhrs,bshd->brhd", attention, value_heads, preferred_element_type=jnp.float32
    )
    return mixture.astype(jnp.bfloat16).reshape(
        batch_size * query_rows.shape[1], head_count * head_size
    )


def after(value, *others):
    return lax.optimization_barrier((value,) + others)[0]


def swap_segments(weights, first, count):
    me = lax.axis_index("segment")
    rows, half = (weights.shape[2], weights.shape[3] // 2)
    size = (1, count, rows, half)
    kept = lax.dynamic_slice(weights, (0, first, 0, me * half), size)[0]
    sent = lax.dynamic_slice(weights, (0, first, 0, (1 - me) * half), size)[0]
    other = lax.ppermute(sent, "segment", [(0, 1), (1, 0)])
    encoder = jnp.where(me == 0, kept, other)

    def decoder(*others):
        late_kept, late_other = lax.optimization_barrier((kept, other) + others)[:2]
        return jnp.where(me == 0, late_other, late_kept)

    return (encoder, decoder)


X_PAIRS = [(i, i ^ 1) for i in range(4)]
Y_PAIRS = [(i, i ^ 2) for i in range(4)]


def near(block):
    count = lax.axis_size("shard")
    me = lax.axis_index("shard")
    rows = block.shape[1]
    if count != 4:
        whole = lax.all_gather(block, "shard", axis=1, tiled=True)
        return [(i, 0, whole[:, i * rows : (i + 1) * rows]) for i in range(count)]
    return [
        (me, 0, block),
        (me ^ 1, 0, lax.ppermute(block, "shard", X_PAIRS)),
        (me ^ 2, 0, lax.ppermute(block, "shard", Y_PAIRS)),
    ]


def far(pieces):
    if lax.axis_size("shard") != 4:
        return []
    me = lax.axis_index("shard")
    rows = pieces[0][2].shape[1]
    top = lax.ppermute(pieces[2][2][:, : rows // 2], "shard", X_PAIRS)
    bottom = lax.ppermute(pieces[1][2][:, rows // 2 :], "shard", Y_PAIRS)
    return [(me ^ 3, 0, top), (me ^ 3, rows // 2, bottom)]


def blocks(pieces):
    return [piece[2] for piece in pieces]


def project(rows_in, pieces, shard_rows, total=None):
    for owner, first, block in pieces:
        depth = block.shape[1]
        part = lax.dynamic_slice_in_dim(rows_in, owner * shard_rows + first, depth, axis=1)
        term = jnp.einsum("rn,knh->rkh", part, block, preferred_element_type=jnp.float32)
        total = term if total is None else total + term
    return total


def in_order(pieces, shard_rows):
    columns = pieces[0][2].shape[2]
    whole = jnp.zeros((D, columns), jnp.bfloat16)
    for owner, first, block in pieces:
        whole = lax.dynamic_update_slice_in_dim(whole, block[0], owner * shard_rows + first, axis=0)
    return whole


def body(store_tokens, retrieved, owner_shard, targets, vocab_table, norm_gains, layer_weights):
    shard_count = lax.axis_size("shard")
    my_shard = lax.axis_index("shard")
    enc_qkv, dec_qkv = swap_segments(layer_weights, 0, 3)
    per_question = retrieved.shape[1]
    length = store_tokens.shape[1]
    slot_cap = max(2, (per_question + shard_count - 1) // shard_count)
    owners = owner_shard.reshape(retrieved.shape)
    positions = jnp.arange(per_question)
    before = positions[None, :] < positions[:, None]
    matches = owners[:, :, None] == owners[:, None, :]
    slot_rank = jnp.sum(jnp.where(matches & before[None], 1, 0), axis=2).astype(jnp.int32)
    slot_numbers = jnp.arange(slot_cap)
    chosen = (owners[:, None, :] == my_shard) & (
        slot_rank[:, None, :] == slot_numbers[None, :, None]
    )
    local_rows = jnp.sum(jnp.where(chosen, retrieved[:, None, :], 0), axis=2)
    send_ids = jnp.take(store_tokens, local_rows.reshape(-1), axis=0).reshape(
        shard_count, slot_cap, length
    )
    arrived = lax.all_to_all(send_ids, "shard", split_axis=0, concat_axis=0, tiled=True)
    mine_owner = lax.dynamic_index_in_dim(owners, my_shard, 0, keepdims=False)
    mine_rank = lax.dynamic_index_in_dim(slot_rank, my_shard, 0, keepdims=False)
    arrived_rows = arrived.reshape(shard_count * slot_cap, length)
    passage_ids = jnp.take(arrived_rows, mine_owner * slot_cap + mine_rank, axis=0).reshape(-1)
    enc_out, dec_out = swap_segments(layer_weights, 3, 1)
    shard_rows = layer_weights.shape[2]
    head_block = enc_qkv.shape[2]
    head_count = head_block // DH
    pass_rows = passage_ids.shape[0]
    all_ids = after(jnp.concatenate([passage_ids, targets.reshape(-1)]), enc_qkv)
    embedded_part = jnp.take(vocab_table, all_ids, axis=0)
    piece = lax.all_gather(embedded_part, ("mp", "segment"), axis=1, tiled=True)
    passage_part = embedded_part[:pass_rows]
    target_part = embedded_part[pass_rows:]
    rows_f32 = piece.astype(jnp.float32)
    scale = lax.rsqrt(jnp.sum(rows_f32 * rows_f32, axis=1) / D + epsilon)
    pass_normed = (rows_f32[:pass_rows] * norm_gains[0]).astype(jnp.bfloat16)
    targ_normed = (rows_f32[pass_rows:] * norm_gains[1]).astype(jnp.bfloat16)
    enc_near = near(enc_qkv)
    accum = project(pass_normed, enc_near, shard_rows)
    enc_far = far(enc_near)
    out_near = near(after(enc_out, accum))
    accum = project(pass_normed, enc_far, shard_rows, accum)
    cross_near = near(dec_qkv(*blocks(out_near))[1:3])
    out_far = far(out_near)
    projected = (accum * scale[:pass_rows, None, None]).astype(jnp.bfloat16)
    shaped = projected.reshape(per_question, length, 3, head_block)
    context = attend(shaped[:, :, 0], shaped[:, :, 1], shaped[:, :, 2], head_count)
    enc_partial = lax.dot_general(
        context,
        in_order(out_near + out_far, shard_rows),
        (((1,), (1,)), ((), ())),
        preferred_element_type=jnp.float32,
    ).astype(jnp.bfloat16)
    enc_sum = lax.psum_scatter(
        enc_partial, ("mp", "segment"), scatter_dimension=1, tiled=True
    ).astype(jnp.float32)
    query_rows = lax.all_to_all(
        after(targ_normed, enc_partial), "shard", split_axis=1, concat_axis=0, tiled=True
    )
    query_terms = jnp.dot(query_rows, dec_qkv(enc_partial)[0], preferred_element_type=jnp.float32)
    query_terms = lax.all_to_all(query_terms, "shard", split_axis=0, concat_axis=0, tiled=True)
    targ_accum = jnp.sum(query_terms.reshape(shard_count, -1, head_block), axis=0)
    queries = (targ_accum * scale[pass_rows:, None]).astype(jnp.bfloat16)[None]
    enc_sum = after(enc_sum, queries, *blocks(cross_near))
    encoded = (passage_part.astype(jnp.float32) + enc_sum).astype(jnp.bfloat16)
    whole_encoded = lax.all_gather(encoded, ("mp", "segment"), axis=1, tiled=True)
    cross_far = far(cross_near)
    late_near = near(dec_out(*blocks(cross_far), queries))
    whole_encoded = after(whole_encoded, *blocks(cross_far))
    enc_f32 = whole_encoded.astype(jnp.float32)
    enc_scale = lax.rsqrt(jnp.sum(enc_f32 * enc_f32, axis=1) / D + epsilon)
    enc_normed = (enc_f32 * norm_gains[2]).astype(jnp.bfloat16)
    cross_accum = project(enc_normed, cross_near + cross_far, shard_rows)
    late_far = far([(o, f, after(b, cross_accum)) for o, f, b in late_near])
    key_values = (cross_accum * enc_scale[:, None, None]).astype(jnp.bfloat16)
    dec_context = attend(queries, key_values[None, :, 0], key_values[None, :, 1], head_count)
    dec_partial = lax.dot_general(
        dec_context,
        in_order(late_near + late_far, shard_rows),
        (((1,), (1,)), ((), ())),
        preferred_element_type=jnp.float32,
    ).astype(jnp.bfloat16)
    terms = lax.all_to_all(dec_partial, ("mp", "segment"), split_axis=1, concat_axis=0, tiled=True)
    terms = terms.reshape(-1, target_part.shape[0], target_part.shape[1]).astype(jnp.float32)
    decoded = (target_part.astype(jnp.float32) + jnp.sum(terms, axis=0)).astype(jnp.bfloat16)
    return (encoded, decoded)


def solution(mesh):
    placed = (
        P("shard", None),
        P(),
        P(),
        P("shard", None),
        P(None, ("mp", "segment")),
        P(),
        P("segment", None, "shard", "mp"),
    )
    return jax.shard_map(
        body,
        mesh=mesh,
        in_specs=placed,
        out_specs=(P("shard", ("mp", "segment")), P("shard", ("mp", "segment"))),
        check_vma=False,
    )
```

profile of v0, /device:TPU:0, one launch (start us, length us, event | category | flops | bytes accessed | tf_op | source)
XLA Modules:
  0.0 385.7 jit_solution(14812456501296723791)
XLA Ops:
  7.2 3.8 dynamic-slice_bitcast_fusion
  15.2 4.7 %all-to-all-start = ((s32[4,1,144]{2,1,0:T(1,128)}), s32[4,1,144]{2,1,0:T(1,128)S(1)}, u32[]{:S(2)}, u32[]{:S(2)}) async-start(s32[4,1,144]{2,1,0:T(1,128)} %reshape.285), calls=%async_computation | async-start | bytes 8192 | tf_op jit(solution)/shard_map/all_to_all | solution.py:119
  20.1 4.4 %all-to-all-done = s32[4,1,144]{2,1,0:T(1,128)S(1)} async-done(((s32[4,1,144]{2,1,0:T(1,128)}), s32[4,1,144]{2,1,0:T(1,128)S(1)}, u32[]{:S(2)}, u32[]{:S(2)}) %all-to-all-start) | async-done | bytes 2336 | tf_op jit(solution)/shard_map/all_to_all | solution.py:119
  26.6 5.7 %broadcast_select_fusion = (bf16[3,1024,512]{2,1,0:T(8,128)(2,1)}, bf16[3,1024,512]{2,1,0:T(8,128)(2,1)}) fusion(bf16[3,1024,512]{2,1,0:T(8,128)(2,1)S(1)} %collective-permute-done, pred[]{:T(512)S(6)} %eq.52, bf16[1,4,1024,1024]{3,2,1,0:T(8,128)(2,1)} %param.13, s32[]{:T(128)S(6)} %select_n.144), kind=kLoop, calls=%fused_computation.18 | loop fusion | flops 1572864 | bytes 12582917 | tf_op jit(solution)/shard_map/jit(_where)/select_n | solution.py:41
  32.4 11.2 %gather_fusion.2 = bf16[640,512]{1,0:T(8,128)(2,1)} fusion(bf16[16384,512]{1,0:T(8,128)(2,1)} %param.11, s32[1024]{0:T(1024)S(1)} %pad_clamp_fusion), kind=kCustom, calls=%fused_computation.2 | custom fusion | bytes 1313280 | tf_op jit(solution)/shard_map/jit(_take)/gather | solution.py:130
  43.6 2.1 broadcast_select_fusion.3
  47.2 2.3 dynamic-slice_bitcast_fusion.2
  49.5 3.0 collective-permute-done.5
  52.5 3.0 broadcast_select_fusion.2
  55.5 60.0 %collective-permute-done.2 = bf16[3,1024,512]{2,1,0:T(8,128)(2,1)} collective-permute-done((bf16[3,1024,512]{2,1,0:T(8,128)(2,1)}, bf16[3,1024,512]{2,1,0:T(8,128)(2,1)}, u32[]{:S(2)}, u32[]{:S(2)}) %collective-permute-start.2) | collective-permute-done | bytes 3145760 | tf_op jit(solution)/shard_map/ppermute | solution.py:64
  115.4 2.8 slice.104
  118.8 2.6 slice.105
  122.3 3.9 %convert_element_type.83 = f32[640,4096]{1,0:T(8,128)S(1)} convert(bf16[640,4096]{1,0:T(8,128)(2,1)} %all-gather.3.cloned.1.call-done) | non-fusion elementwise | flops 2621440 | bytes 15728640 | tf_op jit(solution)/shard_map/convert_element_type | solution.py:134
  127.4 2.8 copy-done
  130.2 3.9 %fusion.23 = f32[576,3,512]{2,0,1:T(8,128)S(1)} fusion(bf16[3,1024,512]{2,1,0:T(8,128)(2,1)} %get-tuple-element.32, bf16[576,4096]{1,0:T(8,128)(2,1)S(1)} %fusion.4, s32[]{:T(128)S(6)} %select_n.149), kind=kOutput, calls=%fused_computation.42 | convolution fusion | flops 1811939328 | bytes 7864324 | tf_op jit(solution)/shard_map/rn,knh->rkh/dot_general | solution.py:86
  134.1 4.0 %fusion.21 = f32[576,3,512]{2,0,1:T(8,128)S(1)} fusion(bf16[3,1024,512]{2,1,0:T(8,128)(2,1)} %collective-permute-done.1, bf16[576,4096]{1,0:T(8,128)(2,1)S(1)} %fusion.4, s32[]{:T(128)S(6)} %select_n.150), kind=kOutput, calls=%fused_computation.40 | convolution fusion | flops 1811939328 | bytes 7864324 | tf_op jit(solution)/shard_map/rn,knh->rkh/dot_general | solution.py:86
  138.1 4.1 %add_add_fusion = f32[576,3,512]{2,0,1:T(8,128)S(1)} fusion(f32[576,3,512]{2,0,1:T(8,128)S(1)} %fusion.23, f32[576,3,512]{2,0,1:T(8,128)S(1)} %fusion.21, bf16[3,1024,512]{2,1,0:T(8,128)(2,1)} %collective-permute-done.2, bf16[576,4096]{1,0:T(8,128)(2,1)S(1)} %fusion.4, s32[]{:T(128)S(6)} %select_n.151), kind=kOutput, calls=%fused_computation.15 | convolution fusion | flops 1813708800 | bytes 14942212 | tf_op jit(solution)/shard_map/rn,knh->rkh/dot_general | solution.py:86
  143.5 1.5 collective-permute-start.7
  146.0 9.8 %collective-permute-done.3 = bf16[3,512,512]{2,1,0:T(8,128)(2,1)} collective-permute-done((bf16[3,512,512]{2,1,0:T(8,128)(2,1)}, bf16[3,512,512]{2,1,0:T(8,128)(2,1)}, u32[]{:S(2)}, u32[]{:S(2)}) %collective-permute-start.3) | collective-permute-done | bytes 1572896 | tf_op jit(solution)/shard_map/ppermute | solution.py:73
  155.9 2.5 fusion.53
  159.1 2.7 multiply_convert_fusion
  163.1 2.5 reshape_squeeze.11
  165.5 2.5 reshape_squeeze.10
  168.0 2.5 reshape_squeeze.9
  170.5 2.4 fusion.26
  172.9 4.2 %fusion.85 = (f32[12,8,48]{2,1,0:T(8,128)S(1)}, f32[12,8,48,48]{2,3,1,0:T(8,128)S(1)}) fusion(f32[12,8,48,48]{2,3,1,0:T(8,128)S(1)} %fusion.26), kind=kOutput, calls=%fused_computation.142 | output fusion | flops 884783 | bytes 1787904 | tf_op jit(solution)/shard_map/sub | solution.py:20
  177.8 1.3 copy.61
  179.1 2.7 reshape.234
  182.1 1.3 bitcast_dynamic-update-slice_fusion.5
  184.5 1.5 collective-permute-start.8
  187.7 1.3 bitcast_dynamic-update-slice_fusion.4
  189.1 1.3 bitcast_dynamic-update-slice_fusion.3
  190.4 3.3 collective-permute-done.8
  193.8 2.6 collective-permute-done.9
  196.4 4.3 %convolution_convert_fusion = bf16[576,4096]{1,0:T(8,128)(2,1)} fusion(bf16[576,512]{1,0:T(8,128)(2,1)S(1)} %copy-done.11, bf16[4096,512]{1,0:T(8,128)(2,1)S(1)} %bitcast_dynamic-update-slice_fusion.8), kind=kOutput, calls=%fused_computation.12 | convolution fusion | flops 2418278400 | bytes 9502720 | tf_op jit(solution)/shard_map/dot_general | solution.py:148
  200.7 3.2 slice_select_fusion
  205.3 1.4 fusion.41
  207.5 4.1 %all-to-all-start.1 = ((bf16[64,4,1024]{2,0,1:T(8,128)(2,1)}), bf16[64,4,1024]{2,0,1:T(8,128)(2,1)}, u32[]{:S(2)}, u32[]{:S(2)}) async-start(bf16[64,4,1024]{2,0,1:T(8,128)(2,1)} %bitcast.145), calls=%async_computation.2 | async-start | bytes 1048576 | tf_op jit(solution)/shard_map/all_to_all | solution.py:157
  211.7 38.4 %all-to-all-done.1 = bf16[64,4,1024]{2,0,1:T(8,128)(2,1)} async-done(((bf16[64,4,1024]{2,0,1:T(8,128)(2,1)}), bf16[64,4,1024]{2,0,1:T(8,128)(2,1)}, u32[]{:S(2)}, u32[]{:S(2)}) %all-to-all-start.1) | async-done | bytes 524320 | tf_op jit(solution)/shard_map/all_to_all | solution.py:157
  250.1 2.7 fusion.38
  252.7 3.6 all-to-all-start.2
  256.7 8.7 %all-to-all-done.2 = f32[4,64,512]{2,1,0:T(8,128)S(1)} async-done(((f32[4,64,512]{2,1,0:T(8,128)}), f32[4,64,512]{2,1,0:T(8,128)S(1)}, u32[]{:S(2)}, u32[]{:S(2)}) %all-to-all-start.2) | async-done | bytes 524320 | tf_op jit(solution)/shard_map/all_to_all | solution.py:161
  267.8 1.3 slice.117
  269.1 1.6 collective-permute-start.12
  272.2 14.0 %collective-permute-done.12 = bf16[2,512,512]{2,1,0:T(8,128)(2,1)S(1)} collective-permute-done((bf16[2,512,512]{2,1,0:T(8,128)(2,1)S(1)}, bf16[2,512,512]{2,1,0:T(8,128)(2,1)S(1)}, u32[]{:S(2)}, u32[]{:S(2)}) %collective-permute-start.12) | collective-permute-done | bytes 1048608 | tf_op jit(solution)/shard_map/ppermute | solution.py:73
  286.2 2.4 collective-permute-done.13
  289.7 2.3 broadcast.152
  292.0 2.9 bitcast_dynamic-update-slice_fusion.2
  294.9 1.7 collective-permute-start.15
  296.9 13.1 %collective-permute-done.14 = bf16[1,1024,512]{2,1,0:T(8,128)(2,1)S(1)} collective-permute-done((bf16[1,1024,512]{2,1,0:T(8,128)(2,1)}, bf16[1,1024,512]{2,1,0:T(8,128)(2,1)S(1)}, u32[]{:S(2)}, u32[]{:S(2)}) %collective-permute-start.14) | collective-permute-done | bytes 1048608 | tf_op jit(solution)/shard_map/ppermute | solution.py:63
  312.2 7.9 %all-gather.5.cloned.1.call-done = bf16[576,4096]{1,0:T(8,128)(2,1)} async-done(((bf16[576,512]{1,0:T(8,128)(2,1)}), bf16[576,4096]{1,0:T(8,128)(2,1)}) %all-gather.5.cloned.1.call-update) | async-done | bytes 4718608 | tf_op jit(solution)/shard_map/all_gather | solution.py:166
  320.1 4.3 %fusion.3 = (f32[576]{0:T(1024)S(1)}, bf16[576,4096]{1,0:T(8,128)(2,1)S(1)}) fusion(bf16[576,4096]{1,0:T(8,128)(2,1)} %all-gather.5.cloned.1.call-done, f32[4096]{0:T(1024)S(1)} %bitcast.149), kind=kLoop, calls=%fused_computation.9 | loop fusion | flops 11795904 | bytes 9455872 | tf_op jit(solution)/shard_map/reduce_sum | solution.py:171
  324.4 3.1 fusion.15
  328.3 3.0 fusion.11
  331.3 3.1 fusion.13
  336.8 1.9 slice.94
  338.7 1.5 collective-permute-start.16
  341.0 1.5 collective-permute-start.17
  343.1 1.5 convolution_convert_fusion.3
  344.6 8.5 %collective-permute-done.16 = bf16[1,512,512]{2,1,0:T(8,128)(2,1)} collective-permute-done((bf16[1,512,512]{2,1,0:T(8,128)(2,1)}, bf16[1,512,512]{2,1,0:T(8,128)(2,1)}, u32[]{:S(2)}, u32[]{:S(2)}) %collective-permute-start.16) | collective-permute-done | bytes 524320 | tf_op jit(solution)/shard_map/ppermute | solution.py:73
  353.1 1.9 bitcast_dynamic-update-slice_fusion.7
  355.1 1.9 bitcast_dynamic-update-slice_fusion.6
  357.0 3.6 convolution_convert_fusion.1
  360.7 17.8 %all_to_all.40 = bf16[64,8,512]{2,0,1:T(8,128)(2,1)S(1)} all-to-all(bf16[64,8,512]{2,0,1:T(8,128)(2,1)S(1)} %bitcast.146), channel_id=1, replica_groups=mesh['shard'=4,'mp'=4,'segment'=2] {'mp','segment'}, dimensions={1} | all-to-all | bytes 1048576 | tf_op jit(solution)/shard_map/all_to_all | solution.py:183
  (134 shorter events, 34.2 us)
Async XLA Ops:
  7.2 4.3 %copy-start.13 = (s32[64,48]{0,1:T(8,128)S(1)}, s32[64,48]{0,1:T(8,128)}, u32[]{:S(2)}) copy-start(s32[64,48]{0,1:T(8,128)} %param.7) | copy-start | bytes 36868
  7.2 4.8 %copy-start.16 = (s32[48,1]{0,1:T(1,128)S(1)}, s32[48,1]{0,1:T(1,128)}, u32[]{:S(2)}) copy-start(s32[48,1]{0,1:T(1,128)} %param.9) | copy-start | bytes 580
  7.2 6.1 %copy-start.14 = (s32[4,12]{1,0:T(4,128)S(1)}, s32[4,12]{1,0:T(4,128)}, u32[]{:S(2)}) copy-start(s32[4,12]{1,0:T(4,128)} %param.8) | copy-start | bytes 580
  7.2 19.3 %copy-start.15 = (s32[1,64]{1,0:T(1,128)S(1)}, s32[1,64]{1,0:T(1,128)}, u32[]{:S(2)}) copy-start(s32[1,64]{1,0:T(1,128)} %param.10) | copy-start | bytes 772
  11.0 15.6 %collective-permute-start = (bf16[3,1024,512]{2,1,0:T(8,128)(2,1)}, bf16[3,1024,512]{2,1,0:T(8,128)(2,1)S(1)}, u32[]{:S(2)}, u32[]{:S(2)}) collective-permute-start(bf16[3,1024,512]{2,1,0:T(8,128)(2,1)} %dynamic-slice_bitcast_fusion), channel_id=1, source_target_pairs={{0,1},{1,0},{2,3},{3,2},{4,5},{5,4},{6,7},{7,6},{8,9},{9,8},{10,11... | collective-permute-start | bytes 9437192 | tf_op jit(solution)/shard_map/ppermute | solution.py:40
  15.2 9.4 %all-to-all-start = ((s32[4,1,144]{2,1,0:T(1,128)}), s32[4,1,144]{2,1,0:T(1,128)S(1)}, u32[]{:S(2)}, u32[]{:S(2)}) async-start(s32[4,1,144]{2,1,0:T(1,128)} %reshape.285), calls=%async_computation | async-start | bytes 8192 | tf_op jit(solution)/shard_map/all_to_all | solution.py:119
  19.9 102.4 %all-gather.3.cloned.1.call-start = ((), (), s32[]{:S(2)}) async-start(), calls=%async_computation.5 | async-start | bytes 5898240 | tf_op jit(solution)/shard_map/all_gather | solution.py:131
  43.6 5.8 %copy-start.12 = (f32[3,4096]{1,0:T(4,128)S(1)}, f32[3,4096]{1,0:T(4,128)}, u32[]{:S(2)}) copy-start(f32[3,4096]{1,0:T(4,128)} %param.12) | copy-start | bytes 147460
  45.8 219.7 %reduce-scatter.2.cloned.1.call-start = ((), (), s32[]{:S(2)}) async-start(), calls=%async_computation.6 | async-start | bytes 5308416 | tf_op jit(solution)/shard_map/reduce_scatter | solution.py:154
  46.0 69.5 %collective-permute-start.2 = (bf16[3,1024,512]{2,1,0:T(8,128)(2,1)}, bf16[3,1024,512]{2,1,0:T(8,128)(2,1)}, u32[]{:S(2)}, u32[]{:S(2)}) collective-permute-start(bf16[3,1024,512]{2,1,0:T(8,128)(2,1)} %get-tuple-element.32), channel_id=1, source_target_pairs={{0,16},{8,24},{16,0},{24,8},{1,17},{9,25},{17,1},{25,9},{2,18},{10... | collective-permute-start | bytes 9437192 | tf_op jit(solution)/shard_map/ppermute | solution.py:64
  46.6 72.2 %collective-permute-start.1 = (bf16[3,1024,512]{2,1,0:T(8,128)(2,1)}, bf16[3,1024,512]{2,1,0:T(8,128)(2,1)}, u32[]{:S(2)}, u32[]{:S(2)}) collective-permute-start(bf16[3,1024,512]{2,1,0:T(8,128)(2,1)} %get-tuple-element.32), channel_id=1, source_target_pairs={{0,8},{8,0},{16,24},{24,16},{1,9},{9,1},{17,25},{25,17},{2,10},{10... | collective-permute-start | bytes 9437192 | tf_op jit(solution)/shard_map/ppermute | solution.py:63
  49.5 3.0 collective-permute-start.5
  118.2 37.6 %collective-permute-start.3 = (bf16[3,512,512]{2,1,0:T(8,128)(2,1)}, bf16[3,512,512]{2,1,0:T(8,128)(2,1)}, u32[]{:S(2)}, u32[]{:S(2)}) collective-permute-start(bf16[3,512,512]{2,1,0:T(8,128)(2,1)} %slice.104), channel_id=1, source_target_pairs={{0,8},{8,0},{16,24},{24,16},{1,9},{9,1},{17,25},{25,17},{2,10},{10... | collective-permute-start | bytes 4718600 | tf_op jit(solution)/shard_map/ppermute | solution.py:73
  121.4 37.6 %collective-permute-start.4 = (bf16[3,512,512]{2,1,0:T(8,128)(2,1)}, bf16[3,512,512]{2,1,0:T(8,128)(2,1)}, u32[]{:S(2)}, u32[]{:S(2)}) collective-permute-start(bf16[3,512,512]{2,1,0:T(8,128)(2,1)} %slice.105), channel_id=1, source_target_pairs={{0,16},{8,24},{16,0},{24,8},{1,17},{9,25},{17,1},{25,9},{2,18},{10... | collective-permute-start | bytes 4718600 | tf_op jit(solution)/shard_map/ppermute | solution.py:74
  126.2 4.0 %copy-start = (f32[640,4096]{1,0:T(8,128)}, f32[640,4096]{1,0:T(8,128)S(1)}, u32[]{:S(2)}) copy-start(f32[640,4096]{1,0:T(8,128)S(1)} %convert_element_type.83) | copy-start | bytes 31457284
  134.1 10.9 %slice-start = ((s8[5242880]{0:T(1024)(128)(4,1)}), s8[4194304]{0:T(1024)(128)(4,1)S(1)}, s32[]{:S(2)}) async-start(s8[5242880]{0:T(1024)(128)(4,1)} %bitcast.139), calls=%async_computation.8 | async-start | bytes 8388608
  138.1 6.8 %slice-start.1 = ((s8[5242880]{0:T(1024)(128)(4,1)}), s8[1048576]{0:T(1024)(128)(4,1)S(1)}, s32[]{:S(2)}) async-start(s8[5242880]{0:T(1024)(128)(4,1)} %bitcast.139), calls=%async_computation.9 | async-start | bytes 2097152
  142.2 43.8 %collective-permute-start.6 = (bf16[1,1024,512]{2,1,0:T(8,128)(2,1)}, bf16[1,1024,512]{2,1,0:T(8,128)(2,1)}, u32[]{:S(2)}, u32[]{:S(2)}) collective-permute-start(bf16[1,1024,512]{2,1,0:T(8,128)(2,1)} %get-tuple-element.16), channel_id=1, source_target_pairs={{0,8},{8,0},{16,24},{24,16},{1,9},{9,1},{17,25},{25,17},{2,10},{10... | collective-permute-start | bytes 3145736 | tf_op jit(solution)/shard_map/ppermute | solution.py:63
  143.5 39.9 %collective-permute-start.7 = (bf16[1,1024,512]{2,1,0:T(8,128)(2,1)}, bf16[1,1024,512]{2,1,0:T(8,128)(2,1)}, u32[]{:S(2)}, u32[]{:S(2)}) collective-permute-start(bf16[1,1024,512]{2,1,0:T(8,128)(2,1)} %get-tuple-element.16), channel_id=1, source_target_pairs={{0,16},{8,24},{16,0},{24,8},{1,17},{9,25},{17,1},{25,9},{2,18},{10... | collective-permute-start | bytes 3145736 | tf_op jit(solution)/shard_map/ppermute | solution.py:64
  172.9 4.3 %copy-start.6 = (bf16[12,48,8,64]{3,2,1,0:T(8,128)(2,1)S(1)}, bf16[12,48,8,64]{3,2,1,0:T(8,128)(2,1)}, u32[]{:S(2)}) copy-start(bf16[12,48,8,64]{3,2,1,0:T(8,128)(2,1)} %reshape_squeeze.9) | copy-start | bytes 1769476
  184.5 9.2 %collective-permute-start.8 = (bf16[1,512,512]{2,1,0:T(8,128)(2,1)S(1)}, bf16[1,512,512]{2,1,0:T(8,128)(2,1)S(1)}, u32[]{:S(2)}, u32[]{:S(2)}) collective-permute-start(bf16[1,512,512]{2,1,0:T(8,128)(2,1)S(1)} %slice.109), channel_id=1, source_target_pairs={{0,8},{8,0},{16,24},{24,16},{1,9},{9,1},{17,25},{25,17},{2,10},{10... | collective-permute-start | bytes 1572872 | tf_op jit(solution)/shard_map/ppermute | solution.py:73
  187.1 9.3 %copy-start.11 = (bf16[576,512]{1,0:T(8,128)(2,1)S(1)}, bf16[576,512]{1,0:T(8,128)(2,1)}, u32[]{:S(2)}) copy-start(bf16[576,512]{1,0:T(8,128)(2,1)} %reshape.234) | copy-start | bytes 1769476
  187.1 9.2 %collective-permute-start.9 = (bf16[1,512,512]{2,1,0:T(8,128)(2,1)S(1)}, bf16[1,512,512]{2,1,0:T(8,128)(2,1)S(1)}, u32[]{:S(2)}, u32[]{:S(2)}) collective-permute-start(bf16[1,512,512]{2,1,0:T(8,128)(2,1)S(1)} %slice.110), channel_id=1, source_target_pairs={{0,16},{8,24},{16,0},{24,8},{1,17},{9,25},{17,1},{25,9},{2,18},{10... | collective-permute-start | bytes 1572872 | tf_op jit(solution)/shard_map/ppermute | solution.py:74
  203.9 62.8 %collective-permute-start.10 = (bf16[2,1024,512]{2,1,0:T(8,128)(2,1)}, bf16[2,1024,512]{2,1,0:T(8,128)(2,1)}, u32[]{:S(2)}, u32[]{:S(2)}) collective-permute-start(bf16[2,1024,512]{2,1,0:T(8,128)(2,1)} %slice_select_fusion), channel_id=1, source_target_pairs={{0,8},{8,0},{16,24},{24,16},{1,9},{9,1},{17,25},{25,17},{2,10},{10... | collective-permute-start | bytes 6291464 | tf_op jit(solution)/shard_map/ppermute | solution.py:63
  204.5 62.3 %collective-permute-start.11 = (bf16[2,1024,512]{2,1,0:T(8,128)(2,1)}, bf16[2,1024,512]{2,1,0:T(8,128)(2,1)}, u32[]{:S(2)}, u32[]{:S(2)}) collective-permute-start(bf16[2,1024,512]{2,1,0:T(8,128)(2,1)} %slice_select_fusion), channel_id=1, source_target_pairs={{0,16},{8,24},{16,0},{24,8},{1,17},{9,25},{17,1},{25,9},{2,18},{10... | collective-permute-start | bytes 6291464 | tf_op jit(solution)/shard_map/ppermute | solution.py:64
  207.5 42.5 %all-to-all-start.1 = ((bf16[64,4,1024]{2,0,1:T(8,128)(2,1)}), bf16[64,4,1024]{2,0,1:T(8,128)(2,1)}, u32[]{:S(2)}, u32[]{:S(2)}) async-start(bf16[64,4,1024]{2,0,1:T(8,128)(2,1)} %bitcast.145), calls=%async_computation.2 | async-start | bytes 1048576 | tf_op jit(solution)/shard_map/all_to_all | solution.py:157
  252.7 14.0 %copy-start.1 = (bf16[640,512]{1,0:T(8,128)(2,1)S(1)}, bf16[640,512]{1,0:T(8,128)(2,1)}, u32[]{:S(2)}) copy-start(bf16[640,512]{1,0:T(8,128)(2,1)} %broadcast_select_fusion.3) | copy-start | bytes 1966084
  252.7 12.7 %all-to-all-start.2 = ((f32[4,64,512]{2,1,0:T(8,128)}), f32[4,64,512]{2,1,0:T(8,128)S(1)}, u32[]{:S(2)}, u32[]{:S(2)}) async-start(f32[4,64,512]{2,1,0:T(8,128)} %fusion.38), calls=%async_computation.3 | async-start | bytes 1048576 | tf_op jit(solution)/shard_map/all_to_all | solution.py:161
  256.3 63.8 %all-gather.5.cloned.1.call-start = ((), (), s32[]{:S(2)}) async-start(), calls=%async_computation.7 | async-start | bytes 5308416 | tf_op jit(solution)/shard_map/all_gather | solution.py:166
  269.1 22.9 %copy-start.2 = (bf16[1,1024,512]{2,1,0:T(8,128)(2,1)S(1)}, bf16[1,1024,512]{2,1,0:T(8,128)(2,1)}, u32[]{:S(2)}) copy-start(bf16[1,1024,512]{2,1,0:T(8,128)(2,1)} %get-tuple-element.25) | copy-start | bytes 3145732
  269.1 17.2 %collective-permute-start.12 = (bf16[2,512,512]{2,1,0:T(8,128)(2,1)S(1)}, bf16[2,512,512]{2,1,0:T(8,128)(2,1)S(1)}, u32[]{:S(2)}, u32[]{:S(2)}) collective-permute-start(bf16[2,512,512]{2,1,0:T(8,128)(2,1)S(1)} %slice.117), channel_id=1, source_target_pairs={{0,8},{8,0},{16,24},{24,16},{1,9},{9,1},{17,25},{25,17},{2,10},{10... | collective-permute-start | bytes 3145736 | tf_op jit(solution)/shard_map/ppermute | solution.py:73
  272.0 16.7 %collective-permute-start.13 = (bf16[2,512,512]{2,1,0:T(8,128)(2,1)S(1)}, bf16[2,512,512]{2,1,0:T(8,128)(2,1)S(1)}, u32[]{:S(2)}, u32[]{:S(2)}) collective-permute-start(bf16[2,512,512]{2,1,0:T(8,128)(2,1)S(1)} %slice.118), channel_id=1, source_target_pairs={{0,16},{8,24},{16,0},{24,8},{1,17},{9,25},{17,1},{25,9},{2,18},{10... | collective-permute-start | bytes 3145736 | tf_op jit(solution)/shard_map/ppermute | solution.py:74
  286.2 2.4 copy-start.7
  288.7 1.1 copy-start.9
  294.9 15.0 %collective-permute-start.14 = (bf16[1,1024,512]{2,1,0:T(8,128)(2,1)}, bf16[1,1024,512]{2,1,0:T(8,128)(2,1)S(1)}, u32[]{:S(2)}, u32[]{:S(2)}) collective-permute-start(bf16[1,1024,512]{2,1,0:T(8,128)(2,1)} %get-tuple-element.29), channel_id=1, source_target_pairs={{0,8},{8,0},{16,24},{24,16},{1,9},{9,1},{17,25},{25,17},{2,10},{10... | collective-permute-start | bytes 3145736 | tf_op jit(solution)/shard_map/ppermute | solution.py:63
  294.9 16.1 %collective-permute-start.15 = (bf16[1,1024,512]{2,1,0:T(8,128)(2,1)}, bf16[1,1024,512]{2,1,0:T(8,128)(2,1)S(1)}, u32[]{:S(2)}, u32[]{:S(2)}) collective-permute-start(bf16[1,1024,512]{2,1,0:T(8,128)(2,1)} %get-tuple-element.29), channel_id=1, source_target_pairs={{0,16},{8,24},{16,0},{24,8},{1,17},{9,25},{17,1},{25,9},{2,18},{10... | collective-permute-start | bytes 3145736 | tf_op jit(solution)/shard_map/ppermute | solution.py:64
  309.9 14.5 %copy-start.3 = (bf16[1,1024,512]{2,1,0:T(8,128)(2,1)}, bf16[1,1024,512]{2,1,0:T(8,128)(2,1)S(1)}, u32[]{:S(2)}) copy-start(bf16[1,1024,512]{2,1,0:T(8,128)(2,1)S(1)} %collective-permute-done.14) | copy-start | bytes 3145732
  311.1 13.3 %copy-start.5 = (bf16[1,1024,512]{2,1,0:T(8,128)(2,1)}, bf16[1,1024,512]{2,1,0:T(8,128)(2,1)S(1)}, u32[]{:S(2)}) copy-start(bf16[1,1024,512]{2,1,0:T(8,128)(2,1)S(1)} %collective-permute-done.15) | copy-start | bytes 3145732
  324.4 3.1 copy-start.8
  331.3 3.1 copy-start.10
  335.3 4.8 %copy-start.4 = (bf16[1,1024,512]{2,1,0:T(8,128)(2,1)S(1)}, bf16[1,1024,512]{2,1,0:T(8,128)(2,1)}, u32[]{:S(2)}) copy-start(bf16[1,1024,512]{2,1,0:T(8,128)(2,1)} %copy-done.3) | copy-start | bytes 3145732
  338.7 14.4 %collective-permute-start.16 = (bf16[1,512,512]{2,1,0:T(8,128)(2,1)}, bf16[1,512,512]{2,1,0:T(8,128)(2,1)}, u32[]{:S(2)}, u32[]{:S(2)}) collective-permute-start(bf16[1,512,512]{2,1,0:T(8,128)(2,1)} %slice.94), channel_id=1, source_target_pairs={{0,8},{8,0},{16,24},{24,16},{1,9},{9,1},{17,25},{25,17},{2,10},{10... | collective-permute-start | bytes 1572872 | tf_op jit(solution)/shard_map/ppermute | solution.py:73
  341.0 14.1 %collective-permute-start.17 = (bf16[1,512,512]{2,1,0:T(8,128)(2,1)}, bf16[1,512,512]{2,1,0:T(8,128)(2,1)}, u32[]{:S(2)}, u32[]{:S(2)}) collective-permute-start(bf16[1,512,512]{2,1,0:T(8,128)(2,1)} %slice.95), channel_id=1, source_target_pairs={{0,16},{8,24},{16,0},{24,8},{1,17},{9,25},{17,1},{25,9},{2,18},{10... | collective-permute-start | bytes 1572872 | tf_op jit(solution)/shard_map/ppermute | solution.py:74
Sparse Core Ops, SparseCore 0:
  45.9 55.3 all-gather.2
  200.9 54.6 reduce-scatter.1
  267.9 52.1 all-gather.4
where the time goes:
time: 387 us; the launch traced here: 386 us
  waiting for transfers between devices  177 us (46%)
  local copies, waits for them, and re-layouts  65.8 us (17%)
  matrix products  43.6 us (11%)
  other arithmetic  38.4 us (10%)
  starting transfers between devices  28.8 us (7%)
  blocking collectives  17.8 us (5%)
  between operations  14.3 us (4%)
    ppermute x4, waiting for transfers between devices, near(): lax.ppermute(block, 'shard', Y_PAIRS)  60 us
    all_to_all x1, waiting for transfers between devices, body(): lax.all_to_all(after(targ_normed, enc_partial), 'shard', split_axis=1, co...  38.4 us
    ppermute x4, waiting for transfers between devices, far(): top = lax.ppermute(pieces[2][2][:, :rows // 2], 'shard', X_PAIRS)  35.6 us
    dot_general x10, matrix products, project(): jnp.einsum('rn,knh->rkh', part, block, preferred_element_type=jnp.float32)  28 us
    all_to_all x1, blocking collectives, body(): lax.all_to_all(dec_partial, ('mp', 'segment'), split_axis=1, concat_axis=...  17.8 us
    ppermute x4, waiting for transfers between devices, near(): lax.ppermute(block, 'shard', X_PAIRS)  13.1 us
    gather x1, local copies, waits for them, and re-layouts, body(): embedded_part = jnp.take(vocab_table, all_ids, axis=0)  11.2 us
    dynamic_update_slice x9, local copies, waits for them, and re-layouts, in_order(): lax.dynamic_update_slice_in_dim(whole, block[0], owner * shard_rows + fir...  10.2 us
  transfers between devices with their start and end apart: 24, of which 15 were waited for; matrix products, arithmetic and copies ran while one was open for 24% of the time, Pallas kernels for 0%

commit v1 on v0

--- a/solution.py
+++ b/solution.py
@@ -2,6 +2,7 @@
 import jax.numpy as jnp
 from jax import lax
 from jax.sharding import PartitionSpec as P
+from jax.lax import axis_index, axis_size, ppermute
 
 D = 4096
 DH = 64
@@ -163,7 +164,29 @@
     queries = (targ_accum * scale[pass_rows:, None]).astype(jnp.bfloat16)[None]
     enc_sum = after(enc_sum, queries, *blocks(cross_near))
     encoded = (passage_part.astype(jnp.float32) + enc_sum).astype(jnp.bfloat16)
-    whole_encoded = lax.all_gather(encoded, ("mp", "segment"), axis=1, tiled=True)
+    width = axis_size(("mp", "segment"))
+    by_rank = []
+    dev_i = 0
+    while dev_i < width:
+        by_rank.append((dev_i, (dev_i + 1) % width))
+        dev_i = dev_i + 1
+    entries = []
+    dev_i = 0
+    while dev_i < width:
+        entries.append((dev_i, (dev_i - 1) % width))
+        dev_i = dev_i + 1
+    formed, view_out = ([encoded], [encoded])
+    for _ in range(width // 2):
+        wide_out = ppermute(formed[-1], ("mp", "segment"), by_rank)
+        formed.append(wide_out)
+    no = 0
+    while no < (width - 1) // 2:
+        view_out.append(ppermute(view_out[-1], ("mp", "segment"), entries))
+        no += 1
+    big = jnp.concatenate([*formed[::-1], *view_out[1:]], 1)
+    whole_encoded = jnp.roll(
+        big, (axis_index(("mp", "segment")) - width // 2) * encoded.shape[1], 1
+    )
     cross_far = far(cross_near)
     late_near = near(dec_out(*blocks(cross_far), queries))
     whole_encoded = after(whole_encoded, *blocks(cross_far))

time: 387 us -> 407 us (1.052); the launches traced: 386 us -> 401 us
  starting transfers between devices: 28.8 us -> 37.1 us
  local copies, waits for them, and re-layouts: 65.8 us -> 74 us
    ppermute x0 -> x7, waiting for transfers between devices: none -> 27.9 us  [the longest x3 14.8 us: body(): view_out.append(ppermute(view_out[-1], ('mp', 'segment'), entries))]
    ppermute x4, waiting for transfers between devices: 35.6 us -> 19 us  [far(): top = lax.ppermute(pieces[2][2][:, :rows // 2], 'shard', X_PAIRS)]
    ppermute x4, waiting for transfers between devices: 13.1 us -> 2.15 us  [near(): lax.ppermute(block, 'shard', X_PAIRS)]
    ppermute x0 -> x7, starting transfers between devices: none -> 8.18 us  [the longest x3 8.11 us: body(): view_out.append(ppermute(view_out[-1], ('mp', 'segment'), entries))]
    all_gather x1 -> x0, waiting for transfers between devices: 7.94 us -> none  [body(): lax.all_gather(encoded, ('mp', 'segment'), axis=1, tiled=True)]
    unnamed x42 -> x51, local copies, waits for them, and re-layouts: 5.32 us -> 11.8 us
    ppermute x4, waiting for transfers between devices: 60 us -> 64.6 us  [near(): lax.ppermute(block, 'shard', Y_PAIRS)]
  transfers between devices with their start and end apart: 24 -> 30, of which waited for: 15 -> 19; matrix products, arithmetic and copies ran while one was open for 24% -> 24% of each run, Pallas kernels for 0% -> 0%
where the time goes in v1:
time: 407 us; the launch traced here: 401 us
  waiting for transfers between devices  174 us (43%)
  local copies, waits for them, and re-layouts  74 us (18%)
  matrix products  45.9 us (11%)
  starting transfers between devices  37.1 us (9%)
  other arithmetic  36.1 us (9%)
  blocking collectives  18.7 us (5%)
  between operations  14.9 us (4%)
    ppermute x4, waiting for transfers between devices, near(): lax.ppermute(block, 'shard', Y_PAIRS)  64.6 us
    all_to_all x1, waiting for transfers between devices, body(): lax.all_to_all(after(targ_normed, enc_partial), 'shard', split_axis=1, co...  38.7 us
    dot_general x10, matrix products, project(): jnp.einsum('rn,knh->rkh', part, block, preferred_element_type=jnp.float32)  30.3 us
    ppermute x4, waiting for transfers between devices, far(): top = lax.ppermute(pieces[2][2][:, :rows // 2], 'shard', X_PAIRS)  19 us
    all_to_all x1, blocking collectives, body(): lax.all_to_all(dec_partial, ('mp', 'segment'), split_axis=1, concat_axis=...  18.7 us
    ppermute x3, waiting for transfers between devices, body(): view_out.append(ppermute(view_out[-1], ('mp', 'segment'), entries))  14.8 us
    ppermute x4, waiting for transfers between devices, body(): wide_out = ppermute(formed[-1], ('mp', 'segment'), by_rank)  13.1 us
    unnamed x51, local copies, waits for them, and re-layouts  11.8 us
  transfers between devices with their start and end apart: 30, of which 19 were waited for; matrix products, arithmetic and copies ran while one was open for 24% of the time, Pallas kernels for 0%

profile of v1, /device:TPU:0, one launch (start us, length us, event | category | flops | bytes accessed | tf_op | source)
XLA Modules:
  0.0 401.0 jit_solution(2733511909708295567)
XLA Ops:
  7.2 3.8 dynamic-slice_bitcast_fusion
  15.1 4.7 %all-to-all-start = ((s32[4,1,144]{2,1,0:T(1,128)}), s32[4,1,144]{2,1,0:T(1,128)S(1)}, u32[]{:S(2)}, u32[]{:S(2)}) async-start(s32[4,1,144]{2,1,0:T(1,128)} %reshape.285), calls=%async_computation | async-start | bytes 8192 | tf_op jit(solution)/shard_map/all_to_all | solution.py:120
  20.1 4.4 %all-to-all-done = s32[4,1,144]{2,1,0:T(1,128)S(1)} async-done(((s32[4,1,144]{2,1,0:T(1,128)}), s32[4,1,144]{2,1,0:T(1,128)S(1)}, u32[]{:S(2)}, u32[]{:S(2)}) %all-to-all-start) | async-done | bytes 2336 | tf_op jit(solution)/shard_map/all_to_all | solution.py:120
  26.6 5.7 %broadcast_select_fusion = (bf16[3,1024,512]{2,1,0:T(8,128)(2,1)}, bf16[3,1024,512]{2,1,0:T(8,128)(2,1)}) fusion(bf16[3,1024,512]{2,1,0:T(8,128)(2,1)S(1)} %collective-permute-done, pred[]{:T(512)S(6)} %eq.55, bf16[1,4,1024,1024]{3,2,1,0:T(8,128)(2,1)} %param.13, s32[]{:T(128)S(6)} %select_n.157), kind=kLoop, calls=%fused_computation.18 | loop fusion | flops 1572864 | bytes 12582917 | tf_op jit(solution)/shard_map/jit(_where)/select_n | solution.py:42
  32.3 11.3 %gather_fusion.2 = bf16[640,512]{1,0:T(8,128)(2,1)} fusion(bf16[16384,512]{1,0:T(8,128)(2,1)} %param.11, s32[1024]{0:T(1024)S(1)} %pad_clamp_fusion), kind=kCustom, calls=%fused_computation.2 | custom fusion | bytes 1313280 | tf_op jit(solution)/shard_map/jit(_take)/gather | solution.py:131
  43.6 2.1 broadcast_select_fusion.3
  47.4 2.3 dynamic-slice_bitcast_fusion.2
  49.7 3.0 collective-permute-done.5
  52.7 3.0 broadcast_select_fusion.2
  55.7 60.0 %collective-permute-done.2 = bf16[3,1024,512]{2,1,0:T(8,128)(2,1)} collective-permute-done((bf16[3,1024,512]{2,1,0:T(8,128)(2,1)}, bf16[3,1024,512]{2,1,0:T(8,128)(2,1)}, u32[]{:S(2)}, u32[]{:S(2)}) %collective-permute-start.2) | collective-permute-done | bytes 3145760 | tf_op jit(solution)/shard_map/ppermute | solution.py:65
  115.7 2.8 slice.104
  119.0 2.6 slice.105
  122.5 3.9 convert_element_type.83
  127.6 2.8 copy-done
  130.4 3.9 fusion.23
  134.3 4.0 %fusion.21 = f32[576,3,512]{2,0,1:T(8,128)S(1)} fusion(bf16[3,1024,512]{2,1,0:T(8,128)(2,1)} %collective-permute-done.1, bf16[576,4096]{1,0:T(8,128)(2,1)S(1)} %fusion.4, s32[]{:T(128)S(6)} %select_n.163), kind=kOutput, calls=%fused_computation.40 | convolution fusion | flops 1811939328 | bytes 7864324 | tf_op jit(solution)/shard_map/rn,knh->rkh/dot_general | solution.py:87
  138.4 4.1 %add_add_fusion = f32[576,3,512]{2,0,1:T(8,128)S(1)} fusion(f32[576,3,512]{2,0,1:T(8,128)S(1)} %fusion.23, f32[576,3,512]{2,0,1:T(8,128)S(1)} %fusion.21, bf16[3,1024,512]{2,1,0:T(8,128)(2,1)} %collective-permute-done.2, bf16[576,4096]{1,0:T(8,128)(2,1)S(1)} %fusion.4, s32[]{:T(128)S(6)} %select_n.164), kind=kOutput, calls=%fused_computation.15 | convolution fusion | flops 1813708800 | bytes 14942212 | tf_op jit(solution)/shard_map/rn,knh->rkh/dot_general | solution.py:87
  143.7 1.5 collective-permute-start.7
  146.3 9.8 %collective-permute-done.3 = bf16[3,512,512]{2,1,0:T(8,128)(2,1)} collective-permute-done((bf16[3,512,512]{2,1,0:T(8,128)(2,1)}, bf16[3,512,512]{2,1,0:T(8,128)(2,1)}, u32[]{:S(2)}, u32[]{:S(2)}) %collective-permute-start.3) | collective-permute-done | bytes 1572896 | tf_op jit(solution)/shard_map/ppermute | solution.py:74
  156.1 2.5 fusion.53
  159.3 2.7 multiply_convert_fusion
  163.3 2.6 reshape_squeeze.11
  165.9 2.5 reshape_squeeze.10
  168.4 2.5 reshape_squeeze.9
  170.9 2.4 fusion.26
  173.3 4.2 %fusion.85 = (f32[12,8,48]{2,1,0:T(8,128)S(1)}, f32[12,8,48,48]{2,3,1,0:T(8,128)S(1)}) fusion(f32[12,8,48,48]{2,3,1,0:T(8,128)S(1)} %fusion.26), kind=kOutput, calls=%fused_computation.159 | output fusion | flops 884783 | bytes 1787904 | tf_op jit(solution)/shard_map/sub | solution.py:21
  179.5 2.7 reshape.234
  184.9 1.5 collective-permute-start.8
  190.8 3.3 collective-permute-done.8
  194.2 2.6 collective-permute-done.9
  196.8 4.4 %convolution_convert_fusion = bf16[576,4096]{1,0:T(8,128)(2,1)} fusion(bf16[576,512]{1,0:T(8,128)(2,1)S(1)} %copy-done.7, bf16[4096,512]{1,0:T(8,128)(2,1)S(1)} %bitcast_dynamic-update-slice_fusion.8), kind=kOutput, calls=%fused_computation.12 | convolution fusion | flops 2418278400 | bytes 9502720 | tf_op jit(solution)/shard_map/dot_general | solution.py:149
  201.2 3.2 slice_select_fusion
  205.8 1.4 fusion.41
  208.0 4.2 %all-to-all-start.1 = ((bf16[64,4,1024]{2,0,1:T(8,128)(2,1)}), bf16[64,4,1024]{2,0,1:T(8,128)(2,1)}, u32[]{:S(2)}, u32[]{:S(2)}) async-start(bf16[64,4,1024]{2,0,1:T(8,128)(2,1)} %bitcast.145), calls=%async_computation.2 | async-start | bytes 1048576 | tf_op jit(solution)/shard_map/all_to_all | solution.py:158
  212.2 38.7 %all-to-all-done.1 = bf16[64,4,1024]{2,0,1:T(8,128)(2,1)} async-done(((bf16[64,4,1024]{2,0,1:T(8,128)(2,1)}), bf16[64,4,1024]{2,0,1:T(8,128)(2,1)}, u32[]{:S(2)}, u32[]{:S(2)}) %all-to-all-start.1) | async-done | bytes 524320 | tf_op jit(solution)/shard_map/all_to_all | solution.py:158
  250.8 2.6 fusion.38
  253.5 3.7 all-to-all-start.2
  257.8 8.9 %all-to-all-done.2 = f32[4,64,512]{2,1,0:T(8,128)S(1)} async-done(((f32[4,64,512]{2,1,0:T(8,128)}), f32[4,64,512]{2,1,0:T(8,128)S(1)}, u32[]{:S(2)}, u32[]{:S(2)}) %all-to-all-start.2) | async-done | bytes 524320 | tf_op jit(solution)/shard_map/all_to_all | solution.py:162
  268.0 1.5 collective-permute-start.19
  272.4 11.1 %collective-permute-done.12 = bf16[576,512]{1,0:T(8,128)(2,1)S(1)} collective-permute-done((bf16[576,512]{1,0:T(8,128)(2,1)S(1)}, bf16[576,512]{1,0:T(8,128)(2,1)S(1)}, u32[]{:S(2)}, u32[]{:S(2)}) %collective-permute-start.12) | collective-permute-done | bytes 589856 | tf_op jit(solution)/shard_map/ppermute | solution.py:180
  284.0 2.3 collective-permute-done.20
  286.3 2.2 broadcast.153
  288.6 2.9 bitcast_dynamic-update-slice_fusion.2
  292.7 2.0 collective-permute-done.13
  294.7 2.0 collective-permute-start.22
  297.6 8.5 %collective-permute-done.16 = bf16[576,512]{1,0:T(8,128)(2,1)} collective-permute-done((bf16[576,512]{1,0:T(8,128)(2,1)S(1)}, bf16[576,512]{1,0:T(8,128)(2,1)}, u32[]{:S(2)}, u32[]{:S(2)}) %collective-permute-start.16) | collective-permute-done | bytes 589856 | tf_op jit(solution)/shard_map/ppermute | solution.py:184
  306.1 3.8 collective-permute-start.17
  311.0 2.1 collective-permute-done.21
  314.2 4.6 %collective-permute-done.22 = bf16[1,1024,512]{2,1,0:T(8,128)(2,1)S(1)} collective-permute-done((bf16[1,1024,512]{2,1,0:T(8,128)(2,1)}, bf16[1,1024,512]{2,1,0:T(8,128)(2,1)S(1)}, u32[]{:S(2)}, u32[]{:S(2)}) %collective-permute-start.22) | collective-permute-done | bytes 1048608 | tf_op jit(solution)/shard_map/ppermute | solution.py:65
  319.8 2.7 collective-permute-done.17
  322.5 3.9 collective-permute-start.18
  330.2 3.6 collective-permute-done.18
  338.3 1.9 fusion.3
  340.3 3.0 fusion.15
  343.3 2.0 fusion.47
  345.3 3.0 fusion.11
  348.3 3.0 fusion.13
  351.2 2.1 multiply_convert_fusion.1
  360.3 1.5 convolution_convert_fusion.3
  361.8 5.3 %collective-permute-done.23 = bf16[1,512,512]{2,1,0:T(8,128)(2,1)} collective-permute-done((bf16[1,512,512]{2,1,0:T(8,128)(2,1)}, bf16[1,512,512]{2,1,0:T(8,128)(2,1)}, u32[]{:S(2)}, u32[]{:S(2)}) %collective-permute-start.23) | collective-permute-done | bytes 524320 | tf_op jit(solution)/shard_map/ppermute | solution.py:74
  367.1 1.9 bitcast_dynamic-update-slice_fusion.7
  369.0 1.9 bitcast_dynamic-update-slice_fusion.6
  370.9 3.6 convolution_convert_fusion.1
  374.5 18.7 %all_to_all.40 = bf16[64,8,512]{2,0,1:T(8,128)(2,1)S(1)} all-to-all(bf16[64,8,512]{2,0,1:T(8,128)(2,1)S(1)} %bitcast.146), channel_id=1, replica_groups=mesh['shard'=4,'mp'=4,'segment'=2] {'mp','segment'}, dimensions={1} | all-to-all | bytes 1048576 | tf_op jit(solution)/shard_map/all_to_all | solution.py:206
  (156 shorter events, 52.9 us)
Async XLA Ops:
  7.2 4.3 %copy-start.9 = (s32[64,48]{0,1:T(8,128)S(1)}, s32[64,48]{0,1:T(8,128)}, u32[]{:S(2)}) copy-start(s32[64,48]{0,1:T(8,128)} %param.7) | copy-start | bytes 36868
  7.2 4.8 %copy-start.13 = (s32[48,1]{0,1:T(1,128)S(1)}, s32[48,1]{0,1:T(1,128)}, u32[]{:S(2)}) copy-start(s32[48,1]{0,1:T(1,128)} %param.9) | copy-start | bytes 580
  7.2 6.1 %copy-start.10 = (s32[4,12]{1,0:T(4,128)S(1)}, s32[4,12]{1,0:T(4,128)}, u32[]{:S(2)}) copy-start(s32[4,12]{1,0:T(4,128)} %param.8) | copy-start | bytes 580
  7.2 19.3 %copy-start.12 = (s32[1,64]{1,0:T(1,128)S(1)}, s32[1,64]{1,0:T(1,128)}, u32[]{:S(2)}) copy-start(s32[1,64]{1,0:T(1,128)} %param.10) | copy-start | bytes 772
  11.0 15.6 %collective-permute-start = (bf16[3,1024,512]{2,1,0:T(8,128)(2,1)}, bf16[3,1024,512]{2,1,0:T(8,128)(2,1)S(1)}, u32[]{:S(2)}, u32[]{:S(2)}) collective-permute-start(bf16[3,1024,512]{2,1,0:T(8,128)(2,1)} %dynamic-slice_bitcast_fusion), channel_id=1, source_target_pairs={{0,1},{1,0},{2,3},{3,2},{4,5},{5,4},{6,7},{7,6},{8,9},{9,8},{10,11... | collective-permute-start | bytes 9437192 | tf_op jit(solution)/shard_map/ppermute | solution.py:41
  15.1 9.4 %all-to-all-start = ((s32[4,1,144]{2,1,0:T(1,128)}), s32[4,1,144]{2,1,0:T(1,128)S(1)}, u32[]{:S(2)}, u32[]{:S(2)}) async-start(s32[4,1,144]{2,1,0:T(1,128)} %reshape.285), calls=%async_computation | async-start | bytes 8192 | tf_op jit(solution)/shard_map/all_to_all | solution.py:120
  19.9 102.6 %all-gather.2.cloned.1.call-start = ((), (), s32[]{:S(2)}) async-start(), calls=%async_computation.5 | async-start | bytes 5898240 | tf_op jit(solution)/shard_map/all_gather | solution.py:132
  32.3 17.4 %copy-start.8 = (f32[3,4096]{1,0:T(4,128)S(1)}, f32[3,4096]{1,0:T(4,128)}, u32[]{:S(2)}) copy-start(f32[3,4096]{1,0:T(4,128)} %param.12) | copy-start | bytes 147460
  45.7 225.2 %reduce-scatter.2.cloned.1.call-start = ((), (), s32[]{:S(2)}) async-start(), calls=%async_computation.6 | async-start | bytes 5308416 | tf_op jit(solution)/shard_map/reduce_scatter | solution.py:155
  46.2 69.5 %collective-permute-start.2 = (bf16[3,1024,512]{2,1,0:T(8,128)(2,1)}, bf16[3,1024,512]{2,1,0:T(8,128)(2,1)}, u32[]{:S(2)}, u32[]{:S(2)}) collective-permute-start(bf16[3,1024,512]{2,1,0:T(8,128)(2,1)} %get-tuple-element.32), channel_id=1, source_target_pairs={{0,16},{8,24},{16,0},{24,8},{1,17},{9,25},{17,1},{25,9},{2,18},{10... | collective-permute-start | bytes 9437192 | tf_op jit(solution)/shard_map/ppermute | solution.py:65
  46.8 72.2 %collective-permute-start.1 = (bf16[3,1024,512]{2,1,0:T(8,128)(2,1)}, bf16[3,1024,512]{2,1,0:T(8,128)(2,1)}, u32[]{:S(2)}, u32[]{:S(2)}) collective-permute-start(bf16[3,1024,512]{2,1,0:T(8,128)(2,1)} %get-tuple-element.32), channel_id=1, source_target_pairs={{0,8},{8,0},{16,24},{24,16},{1,9},{9,1},{17,25},{25,17},{2,10},{10... | collective-permute-start | bytes 9437192 | tf_op jit(solution)/shard_map/ppermute | solution.py:64
  49.7 3.0 collective-permute-start.5
  118.4 37.6 %collective-permute-start.3 = (bf16[3,512,512]{2,1,0:T(8,128)(2,1)}, bf16[3,512,512]{2,1,0:T(8,128)(2,1)}, u32[]{:S(2)}, u32[]{:S(2)}) collective-permute-start(bf16[3,512,512]{2,1,0:T(8,128)(2,1)} %slice.104), channel_id=1, source_target_pairs={{0,8},{8,0},{16,24},{24,16},{1,9},{9,1},{17,25},{25,17},{2,10},{10... | collective-permute-start | bytes 4718600 | tf_op jit(solution)/shard_map/ppermute | solution.py:74
  121.7 37.6 %collective-permute-start.4 = (bf16[3,512,512]{2,1,0:T(8,128)(2,1)}, bf16[3,512,512]{2,1,0:T(8,128)(2,1)}, u32[]{:S(2)}, u32[]{:S(2)}) collective-permute-start(bf16[3,512,512]{2,1,0:T(8,128)(2,1)} %slice.105), channel_id=1, source_target_pairs={{0,16},{8,24},{16,0},{24,8},{1,17},{9,25},{17,1},{25,9},{2,18},{10... | collective-permute-start | bytes 4718600 | tf_op jit(solution)/shard_map/ppermute | solution.py:75
  126.4 4.0 copy-start
  134.3 10.9 %slice-start = ((s8[5242880]{0:T(1024)(128)(4,1)}), s8[4194304]{0:T(1024)(128)(4,1)S(1)}, s32[]{:S(2)}) async-start(s8[5242880]{0:T(1024)(128)(4,1)} %bitcast.139), calls=%async_computation.7 | async-start | bytes 8388608
  138.3 6.8 %slice-start.1 = ((s8[5242880]{0:T(1024)(128)(4,1)}), s8[1048576]{0:T(1024)(128)(4,1)S(1)}, s32[]{:S(2)}) async-start(s8[5242880]{0:T(1024)(128)(4,1)} %bitcast.139), calls=%async_computation.8 | async-start | bytes 2097152
  142.5 43.9 %collective-permute-start.6 = (bf16[1,1024,512]{2,1,0:T(8,128)(2,1)}, bf16[1,1024,512]{2,1,0:T(8,128)(2,1)}, u32[]{:S(2)}, u32[]{:S(2)}) collective-permute-start(bf16[1,1024,512]{2,1,0:T(8,128)(2,1)} %get-tuple-element.16), channel_id=1, source_target_pairs={{0,8},{8,0},{16,24},{24,16},{1,9},{9,1},{17,25},{25,17},{2,10},{10... | collective-permute-start | bytes 3145736 | tf_op jit(solution)/shard_map/ppermute | solution.py:64
  143.7 40.1 %collective-permute-start.7 = (bf16[1,1024,512]{2,1,0:T(8,128)(2,1)}, bf16[1,1024,512]{2,1,0:T(8,128)(2,1)}, u32[]{:S(2)}, u32[]{:S(2)}) collective-permute-start(bf16[1,1024,512]{2,1,0:T(8,128)(2,1)} %get-tuple-element.16), channel_id=1, source_target_pairs={{0,16},{8,24},{16,0},{24,8},{1,17},{9,25},{17,1},{25,9},{2,18},{10... | collective-permute-start | bytes 3145736 | tf_op jit(solution)/shard_map/ppermute | solution.py:65
  173.3 4.3 %copy-start.6 = (bf16[12,48,8,64]{3,2,1,0:T(8,128)(2,1)S(1)}, bf16[12,48,8,64]{3,2,1,0:T(8,128)(2,1)}, u32[]{:S(2)}) copy-start(bf16[12,48,8,64]{3,2,1,0:T(8,128)(2,1)} %reshape_squeeze.9) | copy-start | bytes 1769476
  184.9 11.9 %copy-start.7 = (bf16[576,512]{1,0:T(8,128)(2,1)S(1)}, bf16[576,512]{1,0:T(8,128)(2,1)}, u32[]{:S(2)}) copy-start(bf16[576,512]{1,0:T(8,128)(2,1)} %reshape.234) | copy-start | bytes 1769476
  184.9 9.2 %collective-permute-start.8 = (bf16[1,512,512]{2,1,0:T(8,128)(2,1)S(1)}, bf16[1,512,512]{2,1,0:T(8,128)(2,1)S(1)}, u32[]{:S(2)}, u32[]{:S(2)}) collective-permute-start(bf16[1,512,512]{2,1,0:T(8,128)(2,1)S(1)} %slice.109), channel_id=1, source_target_pairs={{0,8},{8,0},{16,24},{24,16},{1,9},{9,1},{17,25},{25,17},{2,10},{10... | collective-permute-start | bytes 1572872 | tf_op jit(solution)/shard_map/ppermute | solution.py:74
  187.5 9.2 %collective-permute-start.9 = (bf16[1,512,512]{2,1,0:T(8,128)(2,1)S(1)}, bf16[1,512,512]{2,1,0:T(8,128)(2,1)S(1)}, u32[]{:S(2)}, u32[]{:S(2)}) collective-permute-start(bf16[1,512,512]{2,1,0:T(8,128)(2,1)S(1)} %slice.110), channel_id=1, source_target_pairs={{0,16},{8,24},{16,0},{24,8},{1,17},{9,25},{17,1},{25,9},{2,18},{10... | collective-permute-start | bytes 1572872 | tf_op jit(solution)/shard_map/ppermute | solution.py:75
  204.3 62.3 %collective-permute-start.11 = (bf16[2,1024,512]{2,1,0:T(8,128)(2,1)}, bf16[2,1024,512]{2,1,0:T(8,128)(2,1)}, u32[]{:S(2)}, u32[]{:S(2)}) collective-permute-start(bf16[2,1024,512]{2,1,0:T(8,128)(2,1)} %slice_select_fusion), channel_id=1, source_target_pairs={{0,16},{8,24},{16,0},{24,8},{1,17},{9,25},{17,1},{25,9},{2,18},{10... | collective-permute-start | bytes 6291464 | tf_op jit(solution)/shard_map/ppermute | solution.py:65
  204.9 64.6 %collective-permute-start.10 = (bf16[2,1024,512]{2,1,0:T(8,128)(2,1)}, bf16[2,1024,512]{2,1,0:T(8,128)(2,1)}, u32[]{:S(2)}, u32[]{:S(2)}) collective-permute-start(bf16[2,1024,512]{2,1,0:T(8,128)(2,1)} %slice_select_fusion), channel_id=1, source_target_pairs={{0,8},{8,0},{16,24},{24,16},{1,9},{9,1},{17,25},{25,17},{2,10},{10... | collective-permute-start | bytes 6291464 | tf_op jit(solution)/shard_map/ppermute | solution.py:64
  208.0 42.8 %all-to-all-start.1 = ((bf16[64,4,1024]{2,0,1:T(8,128)(2,1)}), bf16[64,4,1024]{2,0,1:T(8,128)(2,1)}, u32[]{:S(2)}, u32[]{:S(2)}) async-start(bf16[64,4,1024]{2,0,1:T(8,128)(2,1)} %bitcast.145), calls=%async_computation.2 | async-start | bytes 1048576 | tf_op jit(solution)/shard_map/all_to_all | solution.py:158
  253.5 13.2 %all-to-all-start.2 = ((f32[4,64,512]{2,1,0:T(8,128)}), f32[4,64,512]{2,1,0:T(8,128)S(1)}, u32[]{:S(2)}, u32[]{:S(2)}) async-start(f32[4,64,512]{2,1,0:T(8,128)} %fusion.38), calls=%async_computation.3 | async-start | bytes 1048576 | tf_op jit(solution)/shard_map/all_to_all | solution.py:162
  257.2 15.0 %copy-start.1 = (bf16[640,512]{1,0:T(8,128)(2,1)S(1)}, bf16[640,512]{1,0:T(8,128)(2,1)}, u32[]{:S(2)}) copy-start(bf16[640,512]{1,0:T(8,128)(2,1)} %broadcast_select_fusion.3) | copy-start | bytes 1966084
  268.0 16.1 %collective-permute-start.19 = (bf16[2,512,512]{2,1,0:T(8,128)(2,1)S(1)}, bf16[2,512,512]{2,1,0:T(8,128)(2,1)}, u32[]{:S(2)}, u32[]{:S(2)}) collective-permute-start(bf16[2,512,512]{2,1,0:T(8,128)(2,1)S(1)} %slice.117), channel_id=1, source_target_pairs={{0,8},{8,0},{16,24},{24,16},{1,9},{9,1},{17,25},{25,17},{2,10},{10... | collective-permute-start | bytes 3145736 | tf_op jit(solution)/shard_map/ppermute | solution.py:74
  270.8 15.5 %collective-permute-start.20 = (bf16[2,512,512]{2,1,0:T(8,128)(2,1)S(1)}, bf16[2,512,512]{2,1,0:T(8,128)(2,1)}, u32[]{:S(2)}, u32[]{:S(2)}) collective-permute-start(bf16[2,512,512]{2,1,0:T(8,128)(2,1)S(1)} %slice.118), channel_id=1, source_target_pairs={{0,16},{8,24},{16,0},{24,8},{1,17},{9,25},{17,1},{25,9},{2,18},{10... | collective-permute-start | bytes 3145736 | tf_op jit(solution)/shard_map/ppermute | solution.py:75
  272.2 16.4 %copy-start.3 = (bf16[1,1024,512]{2,1,0:T(8,128)(2,1)S(1)}, bf16[1,1024,512]{2,1,0:T(8,128)(2,1)}, u32[]{:S(2)}) copy-start(bf16[1,1024,512]{2,1,0:T(8,128)(2,1)} %get-tuple-element.25) | copy-start | bytes 3145732
  272.4 64.0 %copy-start.2 = (bf16[576,512]{1,0:T(8,128)(2,1)}, bf16[576,512]{1,0:T(8,128)(2,1)S(1)}, u32[]{:S(2)}) copy-start(bf16[576,512]{1,0:T(8,128)(2,1)S(1)} %add_convert_fusion) | copy-start | bytes 1769476
  272.4 11.2 %collective-permute-start.12 = (bf16[576,512]{1,0:T(8,128)(2,1)S(1)}, bf16[576,512]{1,0:T(8,128)(2,1)S(1)}, u32[]{:S(2)}, u32[]{:S(2)}) collective-permute-start(bf16[576,512]{1,0:T(8,128)(2,1)S(1)} %add_convert_fusion), channel_id=1, source_target_pairs={{0,1},{1,2},{2,3},{3,4},{4,5},{5,6},{6,7},{7,0},{8,9},{9,10},{10,1... | collective-permute-start | bytes 1769480 | tf_op jit(solution)/shard_map/ppermute | solution.py:180
  283.5 7.9 %copy-start.4 = (bf16[576,512]{1,0:T(8,128)(2,1)}, bf16[576,512]{1,0:T(8,128)(2,1)S(1)}, u32[]{:S(2)}) copy-start(bf16[576,512]{1,0:T(8,128)(2,1)S(1)} %collective-permute-done.12) | copy-start | bytes 1769476
  283.5 11.2 %collective-permute-start.13 = (bf16[576,512]{1,0:T(8,128)(2,1)S(1)}, bf16[576,512]{1,0:T(8,128)(2,1)}, u32[]{:S(2)}, u32[]{:S(2)}) collective-permute-start(bf16[576,512]{1,0:T(8,128)(2,1)S(1)} %collective-permute-done.12), channel_id=1, source_target_pairs={{0,1},{1,2},{2,3},{3,4},{4,5},{5,6},{6,7},{7,0},{8,9},{9,10},{10,1... | collective-permute-start | bytes 1769480 | tf_op jit(solution)/shard_map/ppermute | solution.py:180
  286.3 23.6 %copy-start.11 = (f32[64]{0:T(128)S(1)}, f32[64]{0:T(128)}, u32[]{:S(2)}) copy-start(f32[64]{0:T(128)} %slice.86) | copy-start | bytes 772
  291.5 21.7 %collective-permute-start.21 = (bf16[1,1024,512]{2,1,0:T(8,128)(2,1)}, bf16[1,1024,512]{2,1,0:T(8,128)(2,1)S(1)}, u32[]{:S(2)}, u32[]{:S(2)}) collective-permute-start(bf16[1,1024,512]{2,1,0:T(8,128)(2,1)} %get-tuple-element.29), channel_id=1, source_target_pairs={{0,8},{8,0},{16,24},{24,16},{1,9},{9,1},{17,25},{25,17},{2,10},{10... | collective-permute-start | bytes 3145736 | tf_op jit(solution)/shard_map/ppermute | solution.py:64
  292.3 13.8 %collective-permute-start.16 = (bf16[576,512]{1,0:T(8,128)(2,1)S(1)}, bf16[576,512]{1,0:T(8,128)(2,1)}, u32[]{:S(2)}, u32[]{:S(2)}) collective-permute-start(bf16[576,512]{1,0:T(8,128)(2,1)S(1)} %add_convert_fusion), channel_id=1, source_target_pairs={{0,7},{1,0},{2,1},{3,2},{4,3},{5,4},{6,5},{7,6},{8,15},{9,8},{10,9... | collective-permute-start | bytes 1769480 | tf_op jit(solution)/shard_map/ppermute | solution.py:184
  294.7 15.2 %collective-permute-start.14 = (bf16[576,512]{1,0:T(8,128)(2,1)}, bf16[576,512]{1,0:T(8,128)(2,1)}, u32[]{:S(2)}, u32[]{:S(2)}) collective-permute-start(bf16[576,512]{1,0:T(8,128)(2,1)} %collective-permute-done.13), channel_id=1, source_target_pairs={{0,1},{1,2},{2,3},{3,4},{4,5},{5,6},{6,7},{7,0},{8,9},{9,10},{10,1... | collective-permute-start | bytes 1769480 | tf_op jit(solution)/shard_map/ppermute | solution.py:180
  294.7 24.0 %collective-permute-start.22 = (bf16[1,1024,512]{2,1,0:T(8,128)(2,1)}, bf16[1,1024,512]{2,1,0:T(8,128)(2,1)S(1)}, u32[]{:S(2)}, u32[]{:S(2)}) collective-permute-start(bf16[1,1024,512]{2,1,0:T(8,128)(2,1)} %get-tuple-element.29), channel_id=1, source_target_pairs={{0,16},{8,24},{16,0},{24,8},{1,17},{9,25},{17,1},{25,9},{2,18},{10... | collective-permute-start | bytes 3145736 | tf_op jit(solution)/shard_map/ppermute | solution.py:65
  306.1 16.4 %collective-permute-start.17 = (bf16[576,512]{1,0:T(8,128)(2,1)}, bf16[576,512]{1,0:T(8,128)(2,1)S(1)}, u32[]{:S(2)}, u32[]{:S(2)}) collective-permute-start(bf16[576,512]{1,0:T(8,128)(2,1)} %collective-permute-done.16), channel_id=1, source_target_pairs={{0,7},{1,0},{2,1},{3,2},{4,3},{5,4},{6,5},{7,6},{8,15},{9,8},{10,9... | collective-permute-start | bytes 1769480 | tf_op jit(solution)/shard_map/ppermute | solution.py:184
  309.9 16.4 %collective-permute-start.15 = (bf16[576,512]{1,0:T(8,128)(2,1)}, bf16[576,512]{1,0:T(8,128)(2,1)S(1)}, u32[]{:S(2)}, u32[]{:S(2)}) collective-permute-start(bf16[576,512]{1,0:T(8,128)(2,1)} %collective-permute-done.14), channel_id=1, source_target_pairs={{0,1},{1,2},{2,3},{3,4},{4,5},{5,6},{6,7},{7,0},{8,9},{9,10},{10,1... | collective-permute-start | bytes 1769480 | tf_op jit(solution)/shard_map/ppermute | solution.py:180
  313.2 15.6 %copy-start.5 = (bf16[576,512]{1,0:T(8,128)(2,1)S(1)}, bf16[576,512]{1,0:T(8,128)(2,1)}, u32[]{:S(2)}) copy-start(bf16[576,512]{1,0:T(8,128)(2,1)} %copy-done.4) | copy-start | bytes 1769476
  322.5 11.3 %collective-permute-start.18 = (bf16[576,512]{1,0:T(8,128)(2,1)S(1)}, bf16[576,512]{1,0:T(8,128)(2,1)S(1)}, u32[]{:S(2)}, u32[]{:S(2)}) collective-permute-start(bf16[576,512]{1,0:T(8,128)(2,1)S(1)} %collective-permute-done.17), channel_id=1, source_target_pairs={{0,7},{1,0},{2,1},{3,2},{4,3},{5,4},{6,5},{7,6},{8,15},{9,8},{10,9... | collective-permute-start | bytes 1769480 | tf_op jit(solution)/shard_map/ppermute | solution.py:184
  357.6 9.5 %collective-permute-start.23 = (bf16[1,512,512]{2,1,0:T(8,128)(2,1)}, bf16[1,512,512]{2,1,0:T(8,128)(2,1)}, u32[]{:S(2)}, u32[]{:S(2)}) collective-permute-start(bf16[1,512,512]{2,1,0:T(8,128)(2,1)} %slice.94), channel_id=1, source_target_pairs={{0,8},{8,0},{16,24},{24,16},{1,9},{9,1},{17,25},{25,17},{2,10},{10... | collective-permute-start | bytes 1572872 | tf_op jit(solution)/shard_map/ppermute | solution.py:74
  358.4 10.6 %collective-permute-start.24 = (bf16[1,512,512]{2,1,0:T(8,128)(2,1)S(1)}, bf16[1,512,512]{2,1,0:T(8,128)(2,1)}, u32[]{:S(2)}, u32[]{:S(2)}) collective-permute-start(bf16[1,512,512]{2,1,0:T(8,128)(2,1)S(1)} %slice.95), channel_id=1, source_target_pairs={{0,16},{8,24},{16,0},{24,8},{1,17},{9,25},{17,1},{25,9},{2,18},{10... | collective-permute-start | bytes 1572872 | tf_op jit(solution)/shard_map/ppermute | solution.py:75
Sparse Core Ops, SparseCore 0:
  45.8 55.3 all-gather.1
  201.3 54.6 reduce-scatter.1
